TPU v7x, 128 devices: a whole 4x4x4 slice. The times are simulated.
128 devices in a mesh: pool: 8 (over x, core), wide: 8 (over y, z_hi), narrow: 2 (over z_lo).
Axes of the slice: x: 4, y: 4, z: 4 (z_hi: 2, z_lo: 2; z = z_hi * 2 + z_lo), core: 2. Of those that a mesh axis runs over, the one named last changes fastest.
Arguments:
- states: bfloat16 [384, 2560], P('pool'), may hold values from -3 to 3
- gain_in: float32 [2560], replicated, may hold values from 0.1 to 1.9
- w_qkv: bfloat16 [2560, 8, 6, 128], P('narrow', 'wide'), may hold values from -0.125 to 0.125
- q_gain: float32 [128], replicated, may hold values from 0.1 to 1.9
- k_gain: float32 [128], replicated, may hold values from 0.1 to 1.9
- key_cache: bfloat16 [2304, 8, 128, 128], P('pool', 'wide', 'narrow'), as said below
- value_cache: bfloat16 [2304, 8, 128, 128], P('pool', 'wide', 'narrow'), may hold values from -12 to 12
- cache_len: int32 [384], replicated, may hold values from 1 to 8192, as said below
- page_table: int32 [384, 64], replicated, may hold values from -1 to 2303, as said below
- w_out: bfloat16 [4096, 2560], P('wide'), may hold values from -0.125 to 0.125
- gain_post: float32 [2560], replicated, may hold values from 0.1 to 1.9
- w_gate_up: bfloat16 [2560, 2, 9728], P(None, None, ('wide', 'narrow')), may hold values from -0.125 to 0.125
- w_down: bfloat16 [9728, 2560], P(('wide', 'narrow')), may hold values from -0.078125 to 0.078125
Outputs:
- attn_mixed: bfloat16 [384, 2560], P('pool')
- layer_out: bfloat16 [384, 2560], P('pool')
Inputs may be any that keep to these rules, and one draw needn't show every extreme that they name: `cache_len`: exactly one request has 8192 cached tokens; every other request has at most (5) * 128. `page_table`: entry (r, b) is pool device times 288 plus slot of the page with tokens b * 128 to (b + 1) * 128 - 1 of request r for b < ceil(cache_len[r] / 128), and -1 for later b; no slot is named twice. One pool device holds exactly 288 pages; the others hold the remaining pages, within one page of each other. `key_cache`: cached keys.
All inputs are finite; a program needn't handle non-finite values.
Results may differ from a plain program's by a relative error of at most 0.012.
The roundings to bfloat16 on the way count: a program that leaves them out, or rounds other values in their place, can miss the bound.
Values may be sent and summed in bfloat16 or wider, within the bound.
No kernel may reach another device: no remote copies, remote signals or barrier semaphores. Data moves between devices by JAX's collectives and lax.ppermute only.
A program may use at most 128 MiB of HBM per device.

v0:
```python
import math
import jax
import jax.numpy as jnp
from jax import lax
from jax.sharding import PartitionSpec as P

epsilon = 1e-06
rope_base = 1000000.0
masked_score = -1e30


def rms_scale(values, gain):
    return values * lax.rsqrt(jnp.mean(values * values, axis=-1, keepdims=True) + epsilon) * gain


def rotate(values, angle_pos):
    half = values.shape[-1] // 2
    ramp = jnp.arange(half).astype(jnp.float32)
    freqs = jnp.exp(ramp * (-2.0 * math.log(rope_base) / values.shape[-1]))
    angle = angle_pos[..., None] * freqs
    cosine = jnp.cos(angle)
    sine = jnp.sin(angle)
    lower = values[..., :half]
    upper = values[..., half:]
    return jnp.concatenate([lower * cosine - upper * sine, upper * cosine + lower * sine], axis=-1)


def feed_forward(normed_post, w_gate_up):
    gate_up = jnp.einsum("rd,dcf->rcf", normed_post, w_gate_up, preferred_element_type=jnp.float32)
    return (jax.nn.silu(gate_up[:, 0]) * gate_up[:, 1]).astype(jnp.bfloat16)


def per_device(
    states,
    gain_in,
    w_qkv,
    q_gain,
    k_gain,
    key_cache,
    value_cache,
    cache_len,
    page_table,
    w_out,
    gain_post,
    w_gate_up,
    w_down,
):
    kv_local = w_qkv.shape[1]
    group = w_qkv.shape[2] - 2
    head_dim = w_qkv.shape[3]
    scale = head_dim ** (-0.5)
    narrow_size = lax.axis_size("narrow")
    narrow_index = lax.axis_index("narrow")
    pool_index = lax.axis_index("pool")
    resid_in = states.astype(jnp.float32)
    normed = rms_scale(resid_in, gain_in).astype(jnp.bfloat16)
    part_width = w_qkv.shape[0]
    own_part = lax.dynamic_slice_in_dim(normed, narrow_index * part_width, part_width, 1)
    partial_proj = jnp.einsum("rd,dkch->rkch", own_part, w_qkv, preferred_element_type=jnp.float32)
    proj = lax.psum_scatter(partial_proj, "narrow", scatter_dimension=0, tiled=True)
    row_count = proj.shape[0]
    first_row = (pool_index * narrow_size + narrow_index) * row_count
    own_len = lax.dynamic_slice_in_dim(cache_len, first_row, row_count, 0)
    position = own_len.astype(jnp.float32)
    query = rotate(
        rms_scale(proj[:, :, :group], q_gain),
        jnp.broadcast_to(position[:, None, None], (row_count, kv_local, group)),
    ).astype(jnp.bfloat16)
    key_new = rotate(rms_scale(proj[:, :, group], k_gain), position[:, None]).astype(jnp.bfloat16)
    value_new = proj[:, :, group + 1].astype(jnp.bfloat16)
    all_queries = lax.all_gather(query, ("pool", "narrow"), axis=0, tiled=True)
    slot_count = key_cache.shape[0]
    half_page = key_cache.shape[2]
    holder_count = lax.axis_size("pool")
    req_count = page_table.shape[0]
    max_blocks = page_table.shape[1]
    flat_pages = page_table.reshape(-1)
    entry = jnp.arange(req_count * max_blocks, dtype=jnp.int32)
    target = jnp.where(flat_pages >= 0, flat_pages, holder_count * slot_count)
    owner_all = (
        jnp.full((holder_count * slot_count,), -1, jnp.int32)
        .at[target]
        .set(entry // max_blocks, mode="drop")
    )
    block_all = (
        jnp.zeros((holder_count * slot_count,), jnp.int32)
        .at[target]
        .set(entry % max_blocks, mode="drop")
    )
    owner = lax.dynamic_slice_in_dim(owner_all, pool_index * slot_count, slot_count, 0)
    block = lax.dynamic_slice_in_dim(block_all, pool_index * slot_count, slot_count, 0)
    safe_owner = jnp.maximum(owner, 0)
    page_len = half_page * narrow_size
    token_pos = (
        block[:, None] * page_len
        + narrow_index * half_page
        + jnp.arange(half_page, dtype=jnp.int32)[None, :]
    )
    live = (owner[:, None] >= 0) & (token_pos < cache_len[safe_owner][:, None])
    live_mask = live[:, None, None, :]
    slot_query = all_queries[safe_owner]
    scores = (
        jnp.einsum("skgd,sktd->skgt", slot_query, key_cache, preferred_element_type=jnp.float32)
        * scale
    )
    slot_top = jnp.max(jnp.where(live_mask, scores, masked_score), axis=-1)
    member = owner[:, None] == jnp.arange(req_count, dtype=jnp.int32)[None, :]
    req_top = jnp.max(jnp.where(member[:, :, None, None], slot_top[:, None], masked_score), axis=0)
    expo = jnp.where(live_mask, jnp.exp(scores - req_top[safe_owner][..., None]), 0.0)
    slot_total = jnp.sum(expo, axis=-1)
    slot_out = jnp.einsum(
        "skgt,sktd->skgd",
        expo.astype(jnp.bfloat16),
        value_cache,
        preferred_element_type=jnp.float32,
    )
    member_weight = member.astype(jnp.float32)
    req_out = jnp.einsum(
        "sr,sx->rx",
        member_weight,
        slot_out.reshape(slot_count, -1),
        precision=lax.Precision.HIGHEST,
    )
    req_out = req_out.reshape(req_count, kv_local, group, head_dim)
    req_total = jnp.einsum(
        "sr,sx->rx",
        member_weight,
        slot_total.reshape(slot_count, -1),
        precision=lax.Precision.HIGHEST,
    )
    req_total = req_total.reshape(req_count, kv_local, group)
    got_out, got_top, got_total = (
        lax.all_to_all(req_out[None], ("pool", "narrow"), split_axis=1, concat_axis=0, tiled=True),
        lax.all_to_all(req_top[None], ("pool", "narrow"), split_axis=1, concat_axis=0, tiled=True),
        lax.all_to_all(
            req_total[None], ("pool", "narrow"), split_axis=1, concat_axis=0, tiled=True
        ),
    )
    own_score = (
        jnp.einsum("rkgd,rkd->rkg", query, key_new, preferred_element_type=jnp.float32) * scale
    )
    top = jnp.maximum(jnp.max(got_top, axis=0), own_score)
    factor = jnp.exp(got_top - top[None])
    own_expo = jnp.exp(own_score - top)
    total = jnp.sum(got_total * factor, axis=0) + own_expo
    own_term = jnp.einsum(
        "rkg,rkd->rkgd",
        own_expo.astype(jnp.bfloat16),
        value_new,
        preferred_element_type=jnp.float32,
    )
    summed = jnp.sum(got_out * factor[..., None], axis=0) + own_term
    attn = (
        (summed / total[..., None])
        .astype(jnp.bfloat16)
        .reshape(row_count, kv_local * group * head_dim)
    )
    partial_out = jnp.dot(
        lax.all_gather(attn, "narrow", axis=0, tiled=True),
        w_out,
        preferred_element_type=jnp.float32,
    )
    mixed = lax.psum(partial_out, "wide")
    resid = resid_in + mixed
    attn_mixed = mixed.astype(jnp.bfloat16)
    normed_post = rms_scale(resid, gain_post).astype(jnp.bfloat16)
    hidden = feed_forward(normed_post, w_gate_up)
    down = jnp.dot(hidden, w_down, preferred_element_type=jnp.float32)
    layer_out = (resid + lax.psum(down, ("wide", "narrow"))).astype(jnp.bfloat16)
    return (attn_mixed, layer_out)


def solution(mesh):
    in_specs = (
        P("pool", None),
        P(),
        P("narrow", "wide", None, None),
        P(),
        P(),
        P("pool", "wide", "narrow", None),
        P("pool", "wide", "narrow", None),
        P(),
        P(),
        P("wide", None),
        P(),
        P(None, None, ("wide", "narrow")),
        P(("wide", "narrow"), None),
    )
    out_specs = (P("pool", None), P("pool", None))
    return jax.shard_map(
        per_device, mesh=mesh, in_specs=in_specs, out_specs=out_specs, check_vma=False
    )
```

profile of v0, /device:TPU:0, one launch (start us, length us, event | category | flops | bytes accessed | tf_op | source)
XLA Modules:
  0.0 489.5 jit_solution(1775987561983351854)
XLA Ops:
  7.2 1.2 multiply_reduce_fusion.1
  8.5 1.8 convert_element_type.67
  10.3 0.8 dynamic-slice
  11.0 2.9 fusion.9
  14.0 0.7 fusion.32
  15.1 90.5 %scatter_custom_fusion.1 = s32[2304]{0:T(1024)S(1)} fusion(s32[24576]{0:T(1024)S(1)} %bitcast.105, s32[24576]{0:T(1024)} %fusion.32, s32[]{:T(128)} %constant.29.clone.1), kind=kCustom, calls=%fused_computation.110 | custom fusion | bytes 9728 | tf_op jit(solution)/shard_map/scatter | solution.py:88
  105.6 90.2 %scatter_custom_fusion = s32[2304]{0:T(1024)S(1)} fusion(s32[24576]{0:T(1024)S(1)} %bitcast.106, s32[24576]{0:T(1024)S(1)} %add_select_fusion, s32[]{:T(128)} %constant.28.clone.1), kind=kCustom, calls=%fused_computation.112 | custom fusion | bytes 9220 | tf_op jit(solution)/shard_map/scatter | solution.py:83
  196.0 2.4 gather_fusion
  198.7 0.8 iota_compare_fusion
  199.5 0.8 multiply_reduce_fusion.4
  200.3 0.9 multiply_reduce_fusion.3
  201.2 0.8 multiply_multiply_fusion.1
  202.0 0.7 fusion.76
  202.8 0.9 multiply_multiply_fusion
  203.9 32.0 %all_gather.6 = bf16[384,1,4,128]{3,0,2,1:T(8,128)(2,1)S(1)} all-gather(bf16[24,1,4,128]{3,0,2,1:T(8,128)(2,1)S(1)} %pad_maximum_fusion), channel_id=1, replica_groups=mesh['pool'=8,'wide'=8,'narrow'=2] {'pool','narrow'}, dimensions={0}, use_global_device_ids=true | all-gather | bytes 417792 | tf_op jit(solution)/shard_map/all_gather | solution.py:71
  236.2 2.4 gather_fusion.1
  238.6 5.8 %select_reduce_fusion.1 = (f32[288,4]{1,0:T(8,128)S(1)}, f32[288,4,64]{2,1,0:T(4,128)}) fusion(pred[288,64]{1,0:T(8,128)(4,1)S(1)} %fusion.36, bf16[288,4,128]{2,1,0:T(4,128)(2,1)} %gather_fusion.1, bf16[288,1,64,128]{3,2,1,0:T(8,128)(2,1)} %param.18), kind=kOutput, calls=%fused_computation.23 | convolution fusion | flops 19094400 | bytes 5331456 | tf_op jit(solution)/shard_map/skgd,sktd->skgt/dot_general | solution.py:103
  245.0 0.8 copy.68
  245.8 3.5 all-to-all-start.1
  249.3 1.7 gather_fusion.2
  251.1 1.9 fusion.16
  253.0 4.8 fusion
  257.9 1.4 fusion.29
  259.5 0.8 fusion.58
  260.2 1.3 fusion.70
  261.5 5.6 %all-to-all-start.2 = ((f32[1,384,1,4]{3,2,0,1:T(1,128)}), f32[1,384,1,4]{3,2,0,1:T(1,128)S(1)}, u32[]{:S(2)}, u32[]{:S(2)}) async-start(f32[1,384,1,4]{3,2,0,1:T(1,128)} %bitcast.101), calls=%async_computation.3 | async-start | bytes 393216 | tf_op jit(solution)/shard_map/all_to_all | solution.py:135
  267.2 2.0 convolution_bitcast_fusion
  269.1 1.4 copy.67
  270.5 0.6 reduce_max.32
  271.2 3.5 all-to-all-done.2
  274.7 0.7 copy-done.3
  275.4 4.3 all-to-all-start
  279.7 0.8 multiply_maximum_fusion
  281.1 0.7 subtract_exponential_fusion
  281.8 1.7 copy.69
  283.5 1.0 multiply_reduce_fusion.2
  284.5 0.7 convert_convert_fusion
  285.4 8.9 %all-to-all-done = f32[1,384,1,4,128]{4,3,2,0,1:T(4,128)} async-done(((f32[1,384,1,4,128]{4,3,2,0,1:T(4,128)}), f32[1,384,1,4,128]{4,3,2,0,1:T(4,128)}, u32[]{:S(2)}, u32[]{:S(2)}) %all-to-all-start) | async-done | bytes 786464 | tf_op jit(solution)/shard_map/all_to_all | solution.py:133
  294.3 1.4 fusion.12
  295.7 0.8 copy_bitcast_fusion
  296.5 4.5 all_gather.7
  301.0 3.1 fusion.81
  304.2 85.7 %all-reduce.3.cloned.1.call-done = f32[48,2560]{1,0:T(8,128)} async-done(((f32[48,2560]{1,0:T(8,128)}), f32[48,2560]{1,0:T(8,128)}) %all-reduce.3.cloned.1.call-update) | async-done | bytes 491536 | tf_op jit(solution)/shard_map/psum | solution.py:163
  389.9 1.2 multiply_reduce_fusion
  391.1 4.9 fusion.23
  396.1 1.4 fusion.50
  397.5 83.2 %all-reduce.5.cloned.1.call-done = f32[48,2560]{1,0:T(8,128)} async-done(((f32[48,2560]{1,0:T(8,128)}), f32[48,2560]{1,0:T(8,128)}) %all-reduce.5.cloned.1.call-update) | async-done | bytes 491536 | tf_op jit(solution)/shard_map/psum | solution.py:169
  480.8 2.2 add_convert_fusion
  (70 shorter events, 3.1 us)
Async XLA Ops:
  7.2 388.9 %copy-start = (bf16[608,2560]{1,0:T(8,128)(2,1)S(1)}, bf16[608,2560]{1,0:T(8,128)(2,1)}, u32[]{:S(2)}) copy-start(bf16[608,2560]{1,0:T(8,128)(2,1)} %param.25) | copy-start | bytes 9338884
  7.2 7.4 %copy-start.11 = (s32[384,64]{0,1:T(8,128)S(1)}, s32[384,64]{0,1:T(8,128)}, u32[]{:S(2)}) copy-start(s32[384,64]{0,1:T(8,128)} %param.21) | copy-start | bytes 294916
  7.2 188.8 %copy-start.1 = (s32[384]{0:T(512)S(1)}, s32[384]{0:T(512)}, u32[]{:S(2)}) copy-start(s32[384]{0:T(512)} %param.20) | copy-start | bytes 4612
  7.2 192.3 %reduce-scatter.2.cloned.1.call-start = ((), (), s32[]{:S(2)}) async-start(), calls=%async_computation.4 | async-start | bytes 221184 | tf_op jit(solution)/shard_map/reduce_scatter | solution.py:60
  10.3 192.5 %copy-start.18 = (f32[128]{0:T(128)S(1)}, f32[128]{0:T(128)}, u32[]{:S(2)}) copy-start(f32[128]{0:T(128)} %param.16) | copy-start | bytes 1540
  195.9 40.0 %copy-start.12 = (s32[288]{0:T(512)}, s32[288]{0:T(512)S(1)}, u32[]{:S(2)}) copy-start(s32[288]{0:T(512)S(1)} %get-tuple-element.3) | copy-start | bytes 3460
  195.9 48.5 %copy-start.14 = (s32[1024]{0:T(1024)}, s32[1024]{0:T(1024)S(1)}, u32[]{:S(2)}) copy-start(s32[1024]{0:T(1024)S(1)} %pad_clamp_fusion) | copy-start | bytes 12292
  198.6 45.8 %copy-start.5 = (pred[288,64]{1,0:T(8,128)(4,1)}, pred[288,64]{1,0:T(8,128)(4,1)S(1)}, u32[]{:S(2)}) copy-start(pred[288,64]{1,0:T(8,128)(4,1)S(1)} %fusion.36) | copy-start | bytes 55300
  203.8 32.1 %copy-start.6 = (bf16[24,1,4,64]{3,0,2,1:T(8,128)(2,1)}, bf16[24,1,4,64]{3,0,2,1:T(8,128)(2,1)S(1)}, u32[]{:S(2)}) copy-start(bf16[24,1,4,64]{3,0,2,1:T(8,128)(2,1)S(1)} %get-tuple-element.6) | copy-start | bytes 36868
  203.8 32.1 %copy-start.8 = (bf16[24,1,4,64]{3,0,2,1:T(8,128)(2,1)}, bf16[24,1,4,64]{3,0,2,1:T(8,128)(2,1)S(1)}, u32[]{:S(2)}) copy-start(bf16[24,1,4,64]{3,0,2,1:T(8,128)(2,1)S(1)} %get-tuple-element.7) | copy-start | bytes 36868
  238.6 5.9 %copy-start.4 = (pred[288,384]{1,0:T(8,128)(4,1)S(1)}, pred[288,384]{1,0:T(8,128)(4,1)}, u32[]{:S(2)}) copy-start(pred[288,384]{1,0:T(8,128)(4,1)} %iota_compare_fusion) | copy-start | bytes 331780
  245.8 15.7 %all-to-all-start.1 = ((f32[1,384,1,4]{3,2,0,1:T(1,128)}), f32[1,384,1,4]{3,2,0,1:T(1,128)S(1)}, u32[]{:S(2)}, u32[]{:S(2)}) async-start(f32[1,384,1,4]{3,2,0,1:T(1,128)} %copy.68), calls=%async_computation.2 | async-start | bytes 393216 | tf_op jit(solution)/shard_map/all_to_all | solution.py:134
  252.9 4.9 %copy-start.13 = (s32[288]{0:T(512)S(1)}, s32[288]{0:T(512)}, u32[]{:S(2)}) copy-start(s32[288]{0:T(512)} %copy-done.12) | copy-start | bytes 3460
  253.0 6.3 %copy-start.15 = (bf16[24,64]{1,0:T(8,128)(2,1)S(1)}, bf16[24,64]{1,0:T(8,128)(2,1)}, u32[]{:S(2)}) copy-start(bf16[24,64]{1,0:T(8,128)(2,1)} %get-tuple-element.10) | copy-start | bytes 9220
  253.0 6.3 %copy-start.16 = (bf16[24,64]{1,0:T(8,128)(2,1)S(1)}, bf16[24,64]{1,0:T(8,128)(2,1)}, u32[]{:S(2)}) copy-start(bf16[24,64]{1,0:T(8,128)(2,1)} %get-tuple-element.11) | copy-start | bytes 9220
  253.0 6.4 %copy-start.7 = (bf16[24,1,4,64]{3,0,2,1:T(8,128)(2,1)S(1)}, bf16[24,1,4,64]{3,0,2,1:T(8,128)(2,1)}, u32[]{:S(2)}) copy-start(bf16[24,1,4,64]{3,0,2,1:T(8,128)(2,1)} %copy-done.6) | copy-start | bytes 36868
  253.0 6.4 %copy-start.9 = (bf16[24,1,4,64]{3,0,2,1:T(8,128)(2,1)S(1)}, bf16[24,1,4,64]{3,0,2,1:T(8,128)(2,1)}, u32[]{:S(2)}) copy-start(bf16[24,1,4,64]{3,0,2,1:T(8,128)(2,1)} %copy-done.8) | copy-start | bytes 36868
  261.5 13.2 %all-to-all-start.2 = ((f32[1,384,1,4]{3,2,0,1:T(1,128)}), f32[1,384,1,4]{3,2,0,1:T(1,128)S(1)}, u32[]{:S(2)}, u32[]{:S(2)}) async-start(f32[1,384,1,4]{3,2,0,1:T(1,128)} %bitcast.101), calls=%async_computation.3 | async-start | bytes 393216 | tf_op jit(solution)/shard_map/all_to_all | solution.py:135
  274.7 0.7 copy-start.3
  275.4 19.0 %all-to-all-start = ((f32[1,384,1,4,128]{4,3,2,0,1:T(4,128)}), f32[1,384,1,4,128]{4,3,2,0,1:T(4,128)}, u32[]{:S(2)}, u32[]{:S(2)}) async-start(f32[1,384,1,4,128]{4,3,2,0,1:T(4,128)} %copy.67), calls=%async_computation.1 | async-start | bytes 1572864 | tf_op jit(solution)/shard_map/all_to_all | solution.py:133
  279.6 110.3 %copy-start.2 = (bf16[48,2560]{1,0:T(8,128)(2,1)S(1)}, bf16[48,2560]{1,0:T(8,128)(2,1)}, u32[]{:S(2)}) copy-start(bf16[48,2560]{1,0:T(8,128)(2,1)} %param.13) | copy-start | bytes 737284
  279.7 110.3 %all-reduce.3.cloned.1.call-start = ((), (), s32[]{:S(2)}) async-start(), calls=%async_computation.5 | async-start | bytes 983040 | tf_op jit(solution)/shard_map/psum | solution.py:163
  280.5 0.6 copy-start.10
  284.5 106.7 %copy-start.17 = (f32[2560]{0:T(1024)S(1)}, f32[2560]{0:T(1024)}, u32[]{:S(2)}) copy-start(f32[2560]{0:T(1024)} %param.23) | copy-start | bytes 30724
  304.2 176.6 %all-reduce.5.cloned.1.call-start = ((), (), s32[]{:S(2)}) async-start(), calls=%async_computation.6 | async-start | bytes 983040 | tf_op jit(solution)/shard_map/psum | solution.py:169
Sparse Core Ops, SparseCore 0:
  14.1 15.5 reduce-scatter.1
  304.3 85.5 all-reduce.2
  397.6 83.0 all-reduce.4
where the time goes:
time: 491 us; the launch traced here: 489 us
  local copies, waits for them, and re-layouts  194 us (40%)
  waiting for transfers between devices  181 us (37%)
  blocking collectives  36.5 us (7%)
  matrix products  27.1 us (6%)
  other arithmetic  22.4 us (5%)
  between operations  14.1 us (3%)
  starting transfers between devices  13.6 us (3%)
    scatter x1, local copies, waits for them, and re-layouts, per_device(): block_all = jnp.zeros((holder_count * slot_count,), jnp.int32).at[target]...  90.5 us
    scatter x1, local copies, waits for them, and re-layouts, per_device(): owner_all = jnp.full((holder_count * slot_count,), -1, jnp.int32).at[targ...  90.2 us
    psum x1, waiting for transfers between devices, per_device(): mixed = lax.psum(partial_out, 'wide')  85.7 us
    psum x1, waiting for transfers between devices, per_device(): lax.psum(down, ('wide', 'narrow'))  83.2 us
    all_gather x1, blocking collectives, per_device(): all_queries = lax.all_gather(query, ('pool', 'narrow'), axis=0, tiled=True)  32 us
  transfers between devices with their start and end apart: 6, of which 4 were waited for; matrix products, arithmetic and copies ran while one was open for 42% of the time, Pallas kernels for 0%

commit v1 on v0

--- a/solution.py
+++ b/solution.py
@@ -1,3 +1,4 @@
+import functools
 import math
 import jax
 import jax.numpy as jnp
@@ -7,6 +8,15 @@
 epsilon = 1e-06
 rope_base = 1000000.0
 masked_score = -1e30
+
+
+def number_the_series_all(in_array, ax_name, comm_axis):
+    for dev in (ax_name, comm_axis):
+        in_array = lax.psum(in_array, axis_name=dev)
+    return in_array
+
+
+save_array = functools.partial(number_the_series_all, ax_name="narrow", comm_axis="wide")
 
 
 def rms_scale(values, gain):
@@ -166,7 +176,7 @@
     normed_post = rms_scale(resid, gain_post).astype(jnp.bfloat16)
     hidden = feed_forward(normed_post, w_gate_up)
     down = jnp.dot(hidden, w_down, preferred_element_type=jnp.float32)
-    layer_out = (resid + lax.psum(down, ("wide", "narrow"))).astype(jnp.bfloat16)
+    layer_out = (resid + save_array(down)).astype(jnp.bfloat16)
     return (attn_mixed, layer_out)
 
 

time: 491 us -> 529 us (1.077)
  waiting for transfers between devices: 181 us -> 220 us
    psum x1 -> x2, waiting for transfers between devices: 83.2 us -> 121 us  [number_the_series_all(): in_array = lax.psum(in_array, axis_name=dev)]
  transfers between devices with their start and end apart: 6 -> 7, of which waited for: 4 -> 5; matrix products, arithmetic and copies ran while one was open for 42% -> 39% of each run, Pallas kernels for 0% -> 0%
where the time goes in v1:
time: 529 us; the launch traced here: 528 us
  waiting for transfers between devices  220 us (42%)
  local copies, waits for them, and re-layouts  194 us (37%)
  blocking collectives  36.5 us (7%)
  matrix products  27.1 us (5%)
  other arithmetic  22.4 us (4%)
  between operations  14.1 us (3%)
  starting transfers between devices  13.6 us (3%)
    psum x2, waiting for transfers between devices, number_the_series_all(): in_array = lax.psum(in_array, axis_name=dev)  121 us
    scatter x1, local copies, waits for them, and re-layouts, per_device(): block_all = jnp.zeros((holder_count * slot_count,), jnp.int32).at[target]...  90.5 us
    scatter x1, local copies, waits for them, and re-layouts, per_device(): owner_all = jnp.full((holder_count * slot_count,), -1, jnp.int32).at[targ...  90.2 us
    psum x1, waiting for transfers between devices, per_device(): mixed = lax.psum(partial_out, 'wide')  85.7 us
    all_gather x1, blocking collectives, per_device(): all_queries = lax.all_gather(query, ('pool', 'narrow'), axis=0, tiled=True)  32 us
  transfers between devices with their start and end apart: 7, of which 5 were waited for; matrix products, arithmetic and copies ran while one was open for 39% of the time, Pallas kernels for 0%

profile of v1, /device:TPU:0, one launch (start us, length us, event | category | flops | bytes accessed | tf_op | source)
XLA Modules:
  0.0 527.7 jit_solution(267179423901199933)
XLA Ops:
  7.2 1.2 multiply_reduce_fusion.1
  8.5 1.8 convert_element_type.67
  10.3 0.8 dynamic-slice
  11.0 2.9 fusion.9
  14.0 0.7 fusion.32
  15.1 90.5 %scatter_custom_fusion.1 = s32[2304]{0:T(1024)S(1)} fusion(s32[24576]{0:T(1024)S(1)} %bitcast.105, s32[24576]{0:T(1024)} %fusion.32, s32[]{:T(128)} %constant.29.clone.1), kind=kCustom, calls=%fused_computation.110 | custom fusion | bytes 9728 | tf_op jit(solution)/shard_map/scatter | solution.py:98
  105.6 90.2 %scatter_custom_fusion = s32[2304]{0:T(1024)S(1)} fusion(s32[24576]{0:T(1024)S(1)} %bitcast.106, s32[24576]{0:T(1024)S(1)} %add_select_fusion, s32[]{:T(128)} %constant.28.clone.1), kind=kCustom, calls=%fused_computation.112 | custom fusion | bytes 9220 | tf_op jit(solution)/shard_map/scatter | solution.py:93
  196.0 2.4 gather_fusion
  198.7 0.8 iota_compare_fusion
  199.5 0.8 multiply_reduce_fusion.4
  200.3 0.9 multiply_reduce_fusion.3
  201.2 0.8 multiply_multiply_fusion.1
  202.0 0.7 fusion.76
  202.8 0.9 multiply_multiply_fusion
  203.9 32.0 %all_gather.6 = bf16[384,1,4,128]{3,0,2,1:T(8,128)(2,1)S(1)} all-gather(bf16[24,1,4,128]{3,0,2,1:T(8,128)(2,1)S(1)} %pad_maximum_fusion), channel_id=1, replica_groups=mesh['pool'=8,'wide'=8,'narrow'=2] {'pool','narrow'}, dimensions={0}, use_global_device_ids=true | all-gather | bytes 417792 | tf_op jit(solution)/shard_map/all_gather | solution.py:81
  236.2 2.4 gather_fusion.1
  238.6 5.8 %select_reduce_fusion.1 = (f32[288,4]{1,0:T(8,128)S(1)}, f32[288,4,64]{2,1,0:T(4,128)}) fusion(pred[288,64]{1,0:T(8,128)(4,1)S(1)} %fusion.36, bf16[288,4,128]{2,1,0:T(4,128)(2,1)} %gather_fusion.1, bf16[288,1,64,128]{3,2,1,0:T(8,128)(2,1)} %param.18), kind=kOutput, calls=%fused_computation.23 | convolution fusion | flops 19094400 | bytes 5331456 | tf_op jit(solution)/shard_map/skgd,sktd->skgt/dot_general | solution.py:113
  245.0 0.8 copy.68
  245.8 3.5 all-to-all-start.1
  249.3 1.7 gather_fusion.2
  251.1 1.9 fusion.16
  253.0 4.8 fusion
  257.9 1.4 fusion.29
  259.5 0.8 fusion.58
  260.2 1.3 fusion.70
  261.5 5.6 %all-to-all-start.2 = ((f32[1,384,1,4]{3,2,0,1:T(1,128)}), f32[1,384,1,4]{3,2,0,1:T(1,128)S(1)}, u32[]{:S(2)}, u32[]{:S(2)}) async-start(f32[1,384,1,4]{3,2,0,1:T(1,128)} %bitcast.101), calls=%async_computation.3 | async-start | bytes 393216 | tf_op jit(solution)/shard_map/all_to_all | solution.py:145
  267.2 2.0 convolution_bitcast_fusion
  269.1 1.4 copy.67
  271.2 3.5 all-to-all-done.2
  274.7 0.7 copy-done.3
  275.4 4.3 all-to-all-start
  279.7 0.8 multiply_maximum_fusion
  281.1 0.7 subtract_exponential_fusion
  281.8 1.7 copy.69
  283.5 1.0 multiply_reduce_fusion.2
  284.5 0.7 convert_convert_fusion
  285.4 8.9 %all-to-all-done = f32[1,384,1,4,128]{4,3,2,0,1:T(4,128)} async-done(((f32[1,384,1,4,128]{4,3,2,0,1:T(4,128)}), f32[1,384,1,4,128]{4,3,2,0,1:T(4,128)}, u32[]{:S(2)}, u32[]{:S(2)}) %all-to-all-start) | async-done | bytes 786464 | tf_op jit(solution)/shard_map/all_to_all | solution.py:143
  294.3 1.4 fusion.12
  295.7 0.8 copy_bitcast_fusion
  296.5 4.5 all_gather.7
  301.0 3.1 fusion.81
  304.2 85.7 %all-reduce.4.cloned.1.call-done = f32[48,2560]{1,0:T(8,128)} async-done(((f32[48,2560]{1,0:T(8,128)}), f32[48,2560]{1,0:T(8,128)}) %all-reduce.4.cloned.1.call-update) | async-done | bytes 491536 | tf_op jit(solution)/shard_map/psum | solution.py:173
  389.9 1.2 multiply_reduce_fusion
  391.1 4.9 fusion.23
  396.1 1.4 fusion.50
  397.6 32.3 %all-reduce.6.cloned.1.call-done = f32[48,2560]{1,0:T(8,128)} async-done(((f32[48,2560]{1,0:T(8,128)}), f32[48,2560]{1,0:T(8,128)}) %all-reduce.6.cloned.1.call-update) | async-done | bytes 491536 | tf_op jit(solution)/shard_map/psum | solution.py:15
  429.9 89.1 %all-reduce.8.cloned.1.call-done = f32[48,2560]{1,0:T(8,128)} async-done(((f32[48,2560]{1,0:T(8,128)}), f32[48,2560]{1,0:T(8,128)}) %all-reduce.8.cloned.1.call-update) | async-done | bytes 491536 | tf_op jit(solution)/shard_map/psum | solution.py:15
  519.0 2.2 add_convert_fusion
  (73 shorter events, 3.8 us)
Async XLA Ops:
  7.2 388.9 %copy-start = (bf16[608,2560]{1,0:T(8,128)(2,1)S(1)}, bf16[608,2560]{1,0:T(8,128)(2,1)}, u32[]{:S(2)}) copy-start(bf16[608,2560]{1,0:T(8,128)(2,1)} %param.25) | copy-start | bytes 9338884
  7.2 7.4 %copy-start.11 = (s32[384,64]{0,1:T(8,128)S(1)}, s32[384,64]{0,1:T(8,128)}, u32[]{:S(2)}) copy-start(s32[384,64]{0,1:T(8,128)} %param.21) | copy-start | bytes 294916
  7.2 188.8 %copy-start.1 = (s32[384]{0:T(512)S(1)}, s32[384]{0:T(512)}, u32[]{:S(2)}) copy-start(s32[384]{0:T(512)} %param.20) | copy-start | bytes 4612
  7.2 192.3 %reduce-scatter.2.cloned.1.call-start = ((), (), s32[]{:S(2)}) async-start(), calls=%async_computation.4 | async-start | bytes 221184 | tf_op jit(solution)/shard_map/reduce_scatter | solution.py:70
  10.3 192.5 %copy-start.18 = (f32[128]{0:T(128)S(1)}, f32[128]{0:T(128)}, u32[]{:S(2)}) copy-start(f32[128]{0:T(128)} %param.16) | copy-start | bytes 1540
  195.9 40.0 %copy-start.12 = (s32[288]{0:T(512)}, s32[288]{0:T(512)S(1)}, u32[]{:S(2)}) copy-start(s32[288]{0:T(512)S(1)} %get-tuple-element.3) | copy-start | bytes 3460
  195.9 48.5 %copy-start.14 = (s32[1024]{0:T(1024)}, s32[1024]{0:T(1024)S(1)}, u32[]{:S(2)}) copy-start(s32[1024]{0:T(1024)S(1)} %pad_clamp_fusion) | copy-start | bytes 12292
  198.6 45.8 %copy-start.5 = (pred[288,64]{1,0:T(8,128)(4,1)}, pred[288,64]{1,0:T(8,128)(4,1)S(1)}, u32[]{:S(2)}) copy-start(pred[288,64]{1,0:T(8,128)(4,1)S(1)} %fusion.36) | copy-start | bytes 55300
  203.8 32.1 %copy-start.6 = (bf16[24,1,4,64]{3,0,2,1:T(8,128)(2,1)}, bf16[24,1,4,64]{3,0,2,1:T(8,128)(2,1)S(1)}, u32[]{:S(2)}) copy-start(bf16[24,1,4,64]{3,0,2,1:T(8,128)(2,1)S(1)} %get-tuple-element.6) | copy-start | bytes 36868
  203.8 32.1 %copy-start.8 = (bf16[24,1,4,64]{3,0,2,1:T(8,128)(2,1)}, bf16[24,1,4,64]{3,0,2,1:T(8,128)(2,1)S(1)}, u32[]{:S(2)}) copy-start(bf16[24,1,4,64]{3,0,2,1:T(8,128)(2,1)S(1)} %get-tuple-element.7) | copy-start | bytes 36868
  238.6 5.9 %copy-start.4 = (pred[288,384]{1,0:T(8,128)(4,1)S(1)}, pred[288,384]{1,0:T(8,128)(4,1)}, u32[]{:S(2)}) copy-start(pred[288,384]{1,0:T(8,128)(4,1)} %iota_compare_fusion) | copy-start | bytes 331780
  245.8 15.7 %all-to-all-start.1 = ((f32[1,384,1,4]{3,2,0,1:T(1,128)}), f32[1,384,1,4]{3,2,0,1:T(1,128)S(1)}, u32[]{:S(2)}, u32[]{:S(2)}) async-start(f32[1,384,1,4]{3,2,0,1:T(1,128)} %copy.68), calls=%async_computation.2 | async-start | bytes 393216 | tf_op jit(solution)/shard_map/all_to_all | solution.py:144
  252.9 4.9 copy-start.13
  253.0 6.3 %copy-start.15 = (bf16[24,64]{1,0:T(8,128)(2,1)S(1)}, bf16[24,64]{1,0:T(8,128)(2,1)}, u32[]{:S(2)}) copy-start(bf16[24,64]{1,0:T(8,128)(2,1)} %get-tuple-element.10) | copy-start | bytes 9220
  253.0 6.3 %copy-start.16 = (bf16[24,64]{1,0:T(8,128)(2,1)S(1)}, bf16[24,64]{1,0:T(8,128)(2,1)}, u32[]{:S(2)}) copy-start(bf16[24,64]{1,0:T(8,128)(2,1)} %get-tuple-element.11) | copy-start | bytes 9220
  253.0 6.4 %copy-start.7 = (bf16[24,1,4,64]{3,0,2,1:T(8,128)(2,1)S(1)}, bf16[24,1,4,64]{3,0,2,1:T(8,128)(2,1)}, u32[]{:S(2)}) copy-start(bf16[24,1,4,64]{3,0,2,1:T(8,128)(2,1)} %copy-done.6) | copy-start | bytes 36868
  253.0 6.4 %copy-start.9 = (bf16[24,1,4,64]{3,0,2,1:T(8,128)(2,1)S(1)}, bf16[24,1,4,64]{3,0,2,1:T(8,128)(2,1)}, u32[]{:S(2)}) copy-start(bf16[24,1,4,64]{3,0,2,1:T(8,128)(2,1)} %copy-done.8) | copy-start | bytes 36868
  261.5 13.2 %all-to-all-start.2 = ((f32[1,384,1,4]{3,2,0,1:T(1,128)}), f32[1,384,1,4]{3,2,0,1:T(1,128)S(1)}, u32[]{:S(2)}, u32[]{:S(2)}) async-start(f32[1,384,1,4]{3,2,0,1:T(1,128)} %bitcast.101), calls=%async_computation.3 | async-start | bytes 393216 | tf_op jit(solution)/shard_map/all_to_all | solution.py:145
  274.7 0.7 copy-start.3
  275.4 19.0 %all-to-all-start = ((f32[1,384,1,4,128]{4,3,2,0,1:T(4,128)}), f32[1,384,1,4,128]{4,3,2,0,1:T(4,128)}, u32[]{:S(2)}, u32[]{:S(2)}) async-start(f32[1,384,1,4,128]{4,3,2,0,1:T(4,128)} %copy.67), calls=%async_computation.1 | async-start | bytes 1572864 | tf_op jit(solution)/shard_map/all_to_all | solution.py:143
  279.6 110.3 %copy-start.2 = (bf16[48,2560]{1,0:T(8,128)(2,1)S(1)}, bf16[48,2560]{1,0:T(8,128)(2,1)}, u32[]{:S(2)}) copy-start(bf16[48,2560]{1,0:T(8,128)(2,1)} %param.13) | copy-start | bytes 737284
  279.7 110.3 %all-reduce.4.cloned.1.call-start = ((), (), s32[]{:S(2)}) async-start(), calls=%async_computation.5 | async-start | bytes 983040 | tf_op jit(solution)/shard_map/psum | solution.py:173
  280.5 0.6 copy-start.10
  284.5 106.7 %copy-start.17 = (f32[2560]{0:T(1024)S(1)}, f32[2560]{0:T(1024)}, u32[]{:S(2)}) copy-start(f32[2560]{0:T(1024)} %param.23) | copy-start | bytes 30724
  304.2 125.7 %all-reduce.6.cloned.1.call-start = ((), (), s32[]{:S(2)}) async-start(), calls=%async_computation.6 | async-start | bytes 983040 | tf_op jit(solution)/shard_map/psum | solution.py:15
  397.5 121.5 %all-reduce.8.cloned.1.call-start = ((), (), s32[]{:S(2)}) async-start(), calls=%async_computation.7 | async-start | bytes 983040 | tf_op jit(solution)/shard_map/psum | solution.py:15
Sparse Core Ops, SparseCore 0:
  14.1 15.5 reduce-scatter.1
  304.3 85.5 all-reduce.3
  397.6 32.1 all-reduce.5
  432.4 86.5 all-reduce.7
